TPU v7x, 32 devices: a whole 2x2x4 slice. The times are simulated.
32 devices in a mesh: grp: 2 (over y), keys: 4 (over x, core), qry: 4 (over z).
Axes of the slice: x: 2, y: 2, z: 4, core: 2. Of those that a mesh axis runs over, the one named last changes fastest.
Arguments:
- queries: bfloat16 [4096, 8, 128], P(('grp', 'keys', 'qry')), parts along dimension 0, may hold values from -40 to 40, as said below
- cache_keys: bfloat16 [4096, 128], P(('grp', 'keys')), parts along dimension 0, may hold values from -128 to 128, as said below
- cache_values: bfloat16 [4096, 128], P(('grp', 'keys')), parts along dimension 0, may hold values from -24 to 24
- entry: int32 [8, 4], P(('grp', 'keys'), 'qry'), parts along dimension 0, may hold values from 0 to 3
- visits: int32 [8, 4], P(('grp', 'keys'), 'qry'), parts along dimension 0, may hold values from 3 to 4
- doc_length: int32 [2], P('grp'), parts along dimension 0, may hold values from 1025 to 2048
- slot_params: float32 [2048, 256], P(('grp', 'keys', 'qry')), parts along dimension 0, may hold values from -128 to 128, as said below
- first_moment: float32 [2048, 256], P(('grp', 'keys', 'qry')), parts along dimension 0, may hold values from -3 to 3
- second_moment: float32 [2048, 256], P(('grp', 'keys', 'qry')), parts along dimension 0, may hold values from 0.05 to 1
Outputs:
- teacher_out: bfloat16 [4096, 8, 128], P(('grp', 'keys', 'qry')), parts along dimension 0
- slot_grad: float32 [2048, 256], P(('grp', 'keys', 'qry')), parts along dimension 0
- new_params: float32 [2048, 256], P(('grp', 'keys', 'qry')), parts along dimension 0
- new_first: float32 [2048, 256], P(('grp', 'keys', 'qry')), parts along dimension 0
- new_second: float32 [2048, 256], P(('grp', 'keys', 'qry')), parts along dimension 0
- loss: float32 [2], P('grp'), parts along dimension 0
There are 2 independent parts, one for each index of `grp`. A program takes and returns all parts, laid end to end along the dimension named above; each array names one. Nothing has to cross between parts.
Inputs may be any that keep to these rules, and one draw needn't show every extreme that they name: `queries`: query entries stay within the stated range. `cache_keys`: cache key entries stay within the stated range. `slot_params`: slot entries stay within the stated range.
All inputs are finite; a program needn't handle non-finite values.
Results may differ from a plain program's by a relative error of at most 0.0045.
Values may be sent and summed in bfloat16 or wider, within the bound.
No kernel may reach another device: no remote copies, remote signals or barrier semaphores. Data moves between devices by JAX's collectives and lax.ppermute only.
A program may use at most 64 MiB of HBM per device.

v0:
```python
import math
import jax
import jax.numpy as jnp
from jax import lax
from jax.sharding import PartitionSpec as P

NEG = -1e30


def shifted(block, axis, distance):
    devices = range(lax.axis_size(axis))
    route = [((i - distance) % len(devices), i) for i in devices]
    return lax.ppermute(block, axis, route)


def row_scores(left, right):
    return lax.dot_general(
        left, right, (((1,), (1,)), ((), ())), preferred_element_type=jnp.float32
    )


def attend(state, query_blocks, keys, values, shard, length, score_scale):
    block_width = keys.shape[0]
    place = shard * block_width + lax.iota(jnp.int32, block_width)
    live = (place < length)[None, :]

    def one(block_entry):
        query_portion, big, total, acc = block_entry
        logit_score = jnp.where(live, row_scores(query_portion, keys) * score_scale, NEG)
        new_big = jnp.maximum(big, jnp.max(logit_score, axis=1))
        weight = jnp.where(live, jnp.exp(logit_score - new_big[:, None]), 0.0)
        fade = jnp.exp(big - new_big)
        total = total * fade + jnp.sum(weight, axis=1)
        acc = acc * fade[:, None] + jnp.dot(
            weight.astype(jnp.bfloat16), values, preferred_element_type=jnp.float32
        )
        return (new_big, total, acc)

    big, total, acc = state
    return lax.map(one, (query_blocks, big, total, acc))


def student_tile(loop_state, block_entry, student_keys, student_values, score_scale):
    key_gradient, squared_terms = loop_state
    query_portion, target = block_entry
    logit_score = row_scores(query_portion, student_keys) * score_scale
    peak = jnp.max(logit_score, axis=1, keepdims=True)
    weight = jnp.exp(logit_score - peak)
    prob = weight / jnp.sum(weight, axis=1, keepdims=True)
    block_prob = prob.astype(jnp.bfloat16)
    student_output = jnp.dot(block_prob, student_values, preferred_element_type=jnp.float32)
    diff = student_output - target.astype(jnp.float32)
    squared_terms = squared_terms + jnp.sum(diff * diff)
    block_difference = diff.astype(jnp.bfloat16)
    prob_gradient = row_scores(block_difference, student_values)
    inner = jnp.sum(prob * prob_gradient, axis=1, keepdims=True)
    dscore = (prob * (prob_gradient - inner) * score_scale).astype(jnp.bfloat16)
    dkeys = lax.dot_general(
        dscore, query_portion, (((0,), (0,)), ((), ())), preferred_element_type=jnp.float32
    )
    dvals = lax.dot_general(
        block_prob, block_difference, (((0,), (0,)), ((), ())), preferred_element_type=jnp.float32
    )
    key_gradient = key_gradient + jnp.concatenate([dkeys, dvals], axis=1)
    return ((key_gradient, squared_terms), None)


def body(
    queries,
    cache_keys,
    cache_values,
    entry,
    visits,
    doc_length,
    slot_params,
    first_moment,
    second_moment,
):
    shards = lax.axis_size("keys")
    me = lax.axis_index("keys")
    tok, heads, block_width = queries.shape
    rows = tok * heads
    block = math.gcd(rows, 512)
    nblocks = rows // block
    score_scale = 1.0 / math.sqrt(block_width)
    length = doc_length[0]
    query_blocks = queries.reshape(nblocks, block, block_width)
    start = entry[0, 0]
    count = visits[0, 0]
    state = (
        jnp.full((nblocks, block), NEG, jnp.float32),
        jnp.zeros((nblocks, block), jnp.float32),
        jnp.zeros((nblocks, block, block_width), jnp.float32),
    )

    def visit(step, keys, values, loop_state):
        held = jnp.remainder(me - step, shards)
        go = jnp.remainder(-step - start, shards) < count
        return lax.cond(
            go,
            lambda column_index: attend(
                column_index, query_blocks, keys, values, held, length, score_scale
            ),
            lambda column_index: column_index,
            loop_state,
        )

    def turn(step, loop_state):
        keys, values, big, total, acc = loop_state
        big, total, acc = visit(step, keys, values, (big, total, acc))
        keys, values = shifted((keys, values), "keys", 1)
        return (keys, values, big, total, acc)

    keys, values, big, total, acc = lax.fori_loop(
        0, shards - 1, turn, (cache_keys, cache_values) + state
    )
    big, total, acc = visit(shards - 1, keys, values, (big, total, acc))
    teacher_block_list = (acc / total[:, :, None]).astype(jnp.bfloat16)
    teacher_out = teacher_block_list.reshape(tok, heads, block_width)
    copies = slot_params.astype(jnp.bfloat16)
    complete_sum = lax.all_gather(copies, ("keys", "qry"), axis=0, tiled=True)
    student_keys = complete_sum[:, :block_width]
    student_values = complete_sum[:, block_width:]
    initial_state = (jnp.zeros(complete_sum.shape, jnp.float32), jnp.zeros((), jnp.float32))
    (grad_terms, squared_terms), ignored_value = lax.scan(
        lambda column_index, loop_index: student_tile(
            column_index, loop_index, student_keys, student_values, score_scale
        ),
        initial_state,
        (query_blocks, teacher_block_list),
    )
    slot_grad = lax.psum_scatter(grad_terms, ("keys", "qry"), scatter_dimension=0, tiled=True)
    squares_all = lax.psum(squared_terms, ("keys", "qry"))
    loss = (squares_all / (rows * shards * lax.axis_size("qry"))).reshape(1)
    new_first = 0.9 * first_moment + 0.1 * slot_grad
    new_second = 0.95 * second_moment + 0.05 * slot_grad * slot_grad
    new_params = slot_params - 0.02 * new_first / (jnp.sqrt(new_second) + 1e-08)
    return (teacher_out, slot_grad, new_params, new_first, new_second, loss)


def solution(mesh):
    return jax.shard_map(
        body,
        mesh=mesh,
        in_specs=(
            P(("grp", "keys", "qry"), None, None),
            P(("grp", "keys"), None),
            P(("grp", "keys"), None),
            P(("grp", "keys"), "qry"),
            P(("grp", "keys"), "qry"),
            P("grp"),
            P(("grp", "keys", "qry"), None),
            P(("grp", "keys", "qry"), None),
            P(("grp", "keys", "qry"), None),
        ),
        out_specs=(
            P(("grp", "keys", "qry"), None, None),
            P(("grp", "keys", "qry"), None),
            P(("grp", "keys", "qry"), None),
            P(("grp", "keys", "qry"), None),
            P(("grp", "keys", "qry"), None),
            P("grp"),
        ),
        check_vma=False,
    )
```

profile of v0, /device:TPU:0, one launch (start us, length us, event | category | flops | bytes accessed | tf_op | source)
XLA Modules:
  0.0 162.5 jit_solution(8857728833277977669)
XLA Ops:
  8.6 0.8 convert_element_type.42
  9.5 38.7 %all_gather.3 = bf16[1024,256]{1,0:T(8,128)(2,1)S(1)} all-gather(bf16[64,256]{1,0:T(8,128)(2,1)S(1)} %convert_element_type.42), channel_id=1, replica_groups=mesh['grp'=2,'keys'=4,'qry'=4] {'keys','qry'}, dimensions={0}, use_global_device_ids=true | all-gather | bytes 557056 | tf_op jit(solution)/shard_map/all_gather | solution.py:121
  48.3 32.7 %while.82 = (s32[]{:T(128)}, bf16[512,128]{1,0:T(8,128)(2,1)S(1)}, bf16[512,128]{1,0:T(8,128)(2,1)S(1)}, f32[2,512]{1,0:T(2,128)S(1)}, f32[2,512]{1,0:T(2,128)S(...) while((s32[]{:T(128)}, bf16[512,128]{1,0:T(8,128)(2,1)S(1)}, ...), condition=%wide.region_7.8_spmd, body=%wide.region_0.7_spmd.sunk | while | flops 136711200 | bytes 6747030 | solution.py:114
  49.6 1.7 %collective-permute-start.1 = (bf16[512,128]{1,0:T(8,128)(2,1)}, bf16[512,128]{1,0:T(8,128)(2,1)S(1)}, u32[]{:S(2)}, u32[]{:S(2)}) collective-permute-start(bf16[512,128]{1,0:T(8,128)(2,1)} %copy.56), channel_id=1, source_target_pairs={{12,0},{0,4},{4,8},{8,12},{13,1},{1,5},{5,9},{9,13},{14,2},{2,6},{... | collective-permute-start | bytes 393224 | tf_op jit(solution)/shard_map/while/body/eval_jaxpr/ppermute | solution.py:13
  52.6 7.5 %conditional.4 = ((f32[2,512]{1,0:T(2,128)S(1)}, f32[2,512]{1,0:T(2,128)S(1)}, f32[2,512,128]{2,1,0:T(8,128)S(1)})) conditional(s32[]{:T(128)} %convert_element_type.75, (f32[2,512]{1,0:T(2,128)S(1)}, f32[2,512]{1,0:T(2,128)S(1)}, f32[2,512,128]{2,1,0:T(8,128)S(1)}) %tuple.135, (s32[]{:T(128)}, s32[]{:T(128)}, s32[]{:T(128)}, f32[2,512]{1,0:T(2,128)S(1)}, ...), branch_computations={%region_1.1_spmd, %region_2.6_spmd} | conditional | flops 136711184 | bytes 5173698 | solution.py:99
  52.7 7.4 %while.80 = (s32[]{:T(128)}, f32[2,512]{1,0:T(2,128)S(1)}, f32[2,512]{1,0:T(2,128)S(1)}, f32[2,512,128]{2,1,0:T(8,128)S(1)}, f32[2,512]{1,0:T(2,128)S(1)}, /*ind...) while((s32[]{:T(128)}, f32[2,512]{1,0:T(2,128)S(1)}, ...), condition=%wide.region_6.5_spmd.clone, body=%wide.region_3.4_spmd.clone.sunk | while | flops 136711168 | bytes 4108453 | solution.py:40
  52.7 0.7 compare_reduce_fusion.4
  53.4 1.2 fusion.104
  54.6 1.4 fusion.106
  57.1 1.2 fusion.104
  58.3 1.4 fusion.106
  63.4 7.5 %conditional.4 = ((f32[2,512]{1,0:T(2,128)S(1)}, f32[2,512]{1,0:T(2,128)S(1)}, f32[2,512,128]{2,1,0:T(8,128)S(1)})) conditional(s32[]{:T(128)} %convert_element_type.75, (f32[2,512]{1,0:T(2,128)S(1)}, f32[2,512]{1,0:T(2,128)S(1)}, f32[2,512,128]{2,1,0:T(8,128)S(1)}) %tuple.135, (s32[]{:T(128)}, s32[]{:T(128)}, s32[]{:T(128)}, f32[2,512]{1,0:T(2,128)S(1)}, ...), branch_computations={%region_1.1_spmd, %region_2.6_spmd} | conditional | flops 136711184 | bytes 5173698 | solution.py:99
  63.4 7.4 %while.80 = (s32[]{:T(128)}, f32[2,512]{1,0:T(2,128)S(1)}, f32[2,512]{1,0:T(2,128)S(1)}, f32[2,512,128]{2,1,0:T(8,128)S(1)}, f32[2,512]{1,0:T(2,128)S(1)}, /*ind...) while((s32[]{:T(128)}, f32[2,512]{1,0:T(2,128)S(1)}, ...), condition=%wide.region_6.5_spmd.clone, body=%wide.region_3.4_spmd.clone.sunk | while | flops 136711168 | bytes 4108453 | solution.py:40
  64.1 1.2 fusion.104
  65.4 1.4 fusion.106
  67.8 1.2 fusion.104
  69.0 1.4 fusion.106
  73.5 7.5 %conditional.4 = ((f32[2,512]{1,0:T(2,128)S(1)}, f32[2,512]{1,0:T(2,128)S(1)}, f32[2,512,128]{2,1,0:T(8,128)S(1)})) conditional(s32[]{:T(128)} %convert_element_type.75, (f32[2,512]{1,0:T(2,128)S(1)}, f32[2,512]{1,0:T(2,128)S(1)}, f32[2,512,128]{2,1,0:T(8,128)S(1)}) %tuple.135, (s32[]{:T(128)}, s32[]{:T(128)}, s32[]{:T(128)}, f32[2,512]{1,0:T(2,128)S(1)}, ...), branch_computations={%region_1.1_spmd, %region_2.6_spmd} | conditional | flops 136711184 | bytes 5173698 | solution.py:99
  73.6 7.4 %while.80 = (s32[]{:T(128)}, f32[2,512]{1,0:T(2,128)S(1)}, f32[2,512]{1,0:T(2,128)S(1)}, f32[2,512,128]{2,1,0:T(8,128)S(1)}, f32[2,512]{1,0:T(2,128)S(1)}, /*ind...) while((s32[]{:T(128)}, f32[2,512]{1,0:T(2,128)S(1)}, ...), condition=%wide.region_6.5_spmd.clone, body=%wide.region_3.4_spmd.clone.sunk | while | flops 136711168 | bytes 4108453 | solution.py:40
  74.3 1.2 fusion.104
  75.5 1.4 fusion.106
  77.9 1.2 fusion.104
  79.2 1.4 fusion.106
  81.0 3.8 %conditional.2 = ((f32[2,512]{1,0:T(2,128)S(1)}, f32[2,512,128]{2,1,0:T(8,128)S(1)})) conditional(s32[]{:T(128)} %convert_element_type.40, (f32[2,512]{1,0:T(2,128)S(1)}, f32[2,512,128]{2,1,0:T(8,128)S(1)}) %tuple.70, (s32[]{:T(128)}, s32[]{:T(128)}, f32[2,512]{1,0:T(2,128)S(1)}, f32[2,512]{1,0:T(2,128)S(1)}, bf16[2,512,128]{2,1,0:T(8,128)(2,1)S(1)}, ...), branch_computations={%region_8.9_spmd, %region_9.14_spmd} | conditional | flops 136711184 | bytes 5159334 | solution.py:99
  81.1 3.7 %while.81 = (s32[]{:T(128)}, f32[2,512]{1,0:T(2,128)S(1)}, f32[2,512,128]{2,1,0:T(8,128)S(1)}, f32[2,512]{1,0:T(2,128)S(1)}, f32[2,512]{1,0:T(2,128)S(1)}, /*ind...) while((s32[]{:T(128)}, f32[2,512]{1,0:T(2,128)S(1)}, ...), condition=%wide.region_13.13_spmd.clone, body=%wide.region_10.12_spmd.clone.sunk | while | flops 136711168 | bytes 4102297 | solution.py:40
  85.0 10.0 %while.83 = (s32[]{:T(128)}, f32[1024,256]{0,1:T(8,128)S(1)}, f32[]{:T(128)}, bf16[2,512,128]{2,1,0:T(8,128)(2,1)S(1)}, bf16[1024,128]{1,0:T(8,128)(2,1)S(1)}, /...) while((s32[]{:T(128)}, f32[1024,256]{0,1:T(8,128)S(1)}, ...), condition=%wide.region_19.20_spmd.clone, body=%wide.region_14.19_spmd.clone.sunk | while | flops 680589824 | bytes 26753152 | solution.py:125
  86.6 1.1 multiply_reduce_fusion.7
  91.6 1.1 multiply_reduce_fusion.7
  95.1 1.3 copy.15
  96.4 31.9 %psum.7 = f32[]{:T(128)} all-reduce(f32[]{:T(128)} %get-tuple-element.654), channel_id=1, replica_groups=mesh['grp'=2,'keys'=4,'qry'=4] {'keys','qry'}, use_global_device_ids=true, to_apply=%region_21.22 | all-reduce | flops 1 | bytes 8 | tf_op jit(solution)/shard_map/psum | solution.py:133
  129.0 24.0 %reduce-scatter.2.cloned.1.call-done = f32[64,256]{1,0:T(8,128)} async-done(((f32[1024,256]{1,0:T(8,128)}), f32[64,256]{1,0:T(8,128)}) %reduce-scatter.2.cloned.1.call-update) | async-done | bytes 65552 | tf_op jit(solution)/shard_map/reduce_scatter | solution.py:132
  153.0 1.5 divide_subtract_fusion
  (132 shorter events, 20.4 us)
Async XLA Ops:
  7.2 41.1 %copy-start = (bf16[128,8,128]{2,1,0:T(8,128)(2,1)S(1)}, bf16[128,8,128]{2,1,0:T(8,128)(2,1)}, u32[]{:S(2)}) copy-start(bf16[128,8,128]{2,1,0:T(8,128)(2,1)} %param.21) | copy-start | bytes 786436
  7.2 41.1 %copy-start.1 = (bf16[512,128]{1,0:T(8,128)(2,1)S(1)}, bf16[512,128]{1,0:T(8,128)(2,1)}, u32[]{:S(2)}) copy-start(bf16[512,128]{1,0:T(8,128)(2,1)} %param.22) | copy-start | bytes 393220
  7.2 41.1 %copy-start.2 = (bf16[512,128]{1,0:T(8,128)(2,1)S(1)}, bf16[512,128]{1,0:T(8,128)(2,1)}, u32[]{:S(2)}) copy-start(bf16[512,128]{1,0:T(8,128)(2,1)} %param.23) | copy-start | bytes 393220
  7.2 145.8 %reduce-scatter.2.cloned.1.call-start = ((), (), s32[]{:S(2)}) async-start(), calls=%async_computation.1 | async-start | bytes 1114112 | tf_op jit(solution)/shard_map/reduce_scatter | solution.py:132
  49.0 11.1 %collective-permute-start = (bf16[512,128]{1,0:T(8,128)(2,1)}, bf16[512,128]{1,0:T(8,128)(2,1)S(1)}, u32[]{:S(2)}, u32[]{:S(2)}) collective-permute-start(bf16[512,128]{1,0:T(8,128)(2,1)} %copy.55), channel_id=1, source_target_pairs={{12,0},{0,4},{4,8},{8,12},{13,1},{1,5},{5,9},{9,13},{14,2},{2,6},{... | collective-permute-start | bytes 393224 | tf_op jit(solution)/shard_map/while/body/eval_jaxpr/ppermute | solution.py:13
  49.6 10.5 %collective-permute-start.1 = (bf16[512,128]{1,0:T(8,128)(2,1)}, bf16[512,128]{1,0:T(8,128)(2,1)S(1)}, u32[]{:S(2)}, u32[]{:S(2)}) collective-permute-start(bf16[512,128]{1,0:T(8,128)(2,1)} %copy.56), channel_id=1, source_target_pairs={{12,0},{0,4},{4,8},{8,12},{13,1},{1,5},{5,9},{9,13},{14,2},{2,6},{... | collective-permute-start | bytes 393224 | tf_op jit(solution)/shard_map/while/body/eval_jaxpr/ppermute | solution.py:13
  60.8 10.0 %collective-permute-start = (bf16[512,128]{1,0:T(8,128)(2,1)}, bf16[512,128]{1,0:T(8,128)(2,1)S(1)}, u32[]{:S(2)}, u32[]{:S(2)}) collective-permute-start(bf16[512,128]{1,0:T(8,128)(2,1)} %copy.55), channel_id=1, source_target_pairs={{12,0},{0,4},{4,8},{8,12},{13,1},{1,5},{5,9},{9,13},{14,2},{2,6},{... | collective-permute-start | bytes 393224 | tf_op jit(solution)/shard_map/while/body/eval_jaxpr/ppermute | solution.py:13
  61.5 9.4 %collective-permute-start.1 = (bf16[512,128]{1,0:T(8,128)(2,1)}, bf16[512,128]{1,0:T(8,128)(2,1)S(1)}, u32[]{:S(2)}, u32[]{:S(2)}) collective-permute-start(bf16[512,128]{1,0:T(8,128)(2,1)} %copy.56), channel_id=1, source_target_pairs={{12,0},{0,4},{4,8},{8,12},{13,1},{1,5},{5,9},{9,13},{14,2},{2,6},{... | collective-permute-start | bytes 393224 | tf_op jit(solution)/shard_map/while/body/eval_jaxpr/ppermute | solution.py:13
  71.5 9.5 %collective-permute-start = (bf16[512,128]{1,0:T(8,128)(2,1)}, bf16[512,128]{1,0:T(8,128)(2,1)S(1)}, u32[]{:S(2)}, u32[]{:S(2)}) collective-permute-start(bf16[512,128]{1,0:T(8,128)(2,1)} %copy.55), channel_id=1, source_target_pairs={{12,0},{0,4},{4,8},{8,12},{13,1},{1,5},{5,9},{9,13},{14,2},{2,6},{... | collective-permute-start | bytes 393224 | tf_op jit(solution)/shard_map/while/body/eval_jaxpr/ppermute | solution.py:13
  72.2 8.8 %collective-permute-start.1 = (bf16[512,128]{1,0:T(8,128)(2,1)}, bf16[512,128]{1,0:T(8,128)(2,1)S(1)}, u32[]{:S(2)}, u32[]{:S(2)}) collective-permute-start(bf16[512,128]{1,0:T(8,128)(2,1)} %copy.56), channel_id=1, source_target_pairs={{12,0},{0,4},{4,8},{8,12},{13,1},{1,5},{5,9},{9,13},{14,2},{2,6},{... | collective-permute-start | bytes 393224 | tf_op jit(solution)/shard_map/while/body/eval_jaxpr/ppermute | solution.py:13
  95.0 59.5 %copy-start.3 = (bf16[2,512,128]{2,1,0:T(8,128)(2,1)}, bf16[2,512,128]{2,1,0:T(8,128)(2,1)S(1)}, u32[]{:S(2)}) copy-start(bf16[2,512,128]{2,1,0:T(8,128)(2,1)S(1)} %get-tuple-element.1306) | copy-start | bytes 786436
  95.0 58.0 %copy-start.4 = (f32[64,256]{1,0:T(8,128)S(1)}, f32[64,256]{1,0:T(8,128)}, u32[]{:S(2)}) copy-start(f32[64,256]{1,0:T(8,128)} %param.27) | copy-start | bytes 196612
  95.0 57.9 %copy-start.5 = (f32[64,256]{1,0:T(8,128)S(1)}, f32[64,256]{1,0:T(8,128)}, u32[]{:S(2)}) copy-start(f32[64,256]{1,0:T(8,128)} %param.28) | copy-start | bytes 196612
  95.1 57.9 %copy-start.6 = (f32[64,256]{1,0:T(8,128)S(1)}, f32[64,256]{1,0:T(8,128)}, u32[]{:S(2)}) copy-start(f32[64,256]{1,0:T(8,128)} %param.29) | copy-start | bytes 196612
Sparse Core Ops, SparseCore 0:
  96.5 56.4 reduce-scatter.1
where the time goes:
time: 163 us
  blocking collectives  70.6 us (43%)
  waiting for transfers between devices  24.1 us (15%)
  matrix products  23.3 us (14%)
  between operations  17.3 us (11%)
  other arithmetic  12.6 us (8%)
  loops' own time  6.18 us (4%)
  local copies, waits for them, and re-layouts  6.17 us (4%)
  starting transfers between devices  2.3 us (1%)
    all_gather x1, blocking collectives, body(): complete_sum = lax.all_gather(copies, ('keys', 'qry'), axis=0, tiled=True)  38.7 us
    psum x1, blocking collectives, body(): squares_all = lax.psum(squared_terms, ('keys', 'qry'))  31.9 us
    reduce_scatter x1, waiting for transfers between devices, body(): lax.psum_scatter(grad_terms, ('keys', 'qry'), scatter_dimension=0, tiled=...  24 us
    dot_general x12, matrix products, row_scores(): lax.dot_general(left, right, (((1,), (1,)), ((), ())), preferred_element_...  10.1 us
    dot_general x8, matrix products, one(): jnp.dot(weight.astype(jnp.bfloat16), values, preferred_element_type=jnp.f...  9.39 us
    lt x8, other arithmetic, attend(): live = (place < length)[None, :]  5.37 us
    another operation x1, loops' own time, body(): lax.fori_loop(0, shards - 1, turn, (cache_keys, cache_values) + state)  4.07 us
    another operation x8, local copies, waits for them, and re-layouts  3.92 us
  transfers between devices with their start and end apart: 7, of which 1 were waited for; matrix products, arithmetic and copies ran while one was open for 15% of the time, Pallas kernels for 0%

commit v1 on v0

--- a/solution.py
+++ b/solution.py
@@ -118,7 +118,10 @@
     teacher_block_list = (acc / total[:, :, None]).astype(jnp.bfloat16)
     teacher_out = teacher_block_list.reshape(tok, heads, block_width)
     copies = slot_params.astype(jnp.bfloat16)
-    complete_sum = lax.all_gather(copies, ("keys", "qry"), axis=0, tiled=True)
+    complete_sum = jnp.concatenate(
+        lax.all_to_all(jnp.stack([copies] * lax.axis_size(("keys", "qry"))), ("keys", "qry"), 0, 0),
+        axis=0,
+    )
     student_keys = complete_sum[:, :block_width]
     student_values = complete_sum[:, block_width:]
     initial_state = (jnp.zeros(complete_sum.shape, jnp.float32), jnp.zeros((), jnp.float32))

time: 163 us -> 137 us (0.84)
  blocking collectives: 70.6 us -> 35.4 us
  starting transfers between devices: 2.3 us -> 10.1 us
  local copies, waits for them, and re-layouts: 6.17 us -> 8.09 us
    all_gather x1 -> x0, blocking collectives: 38.7 us -> none  [body(): complete_sum = lax.all_gather(copies, ('keys', 'qry'), axis=0, tiled=True)]
    all_to_all x0 -> x1, starting transfers between devices: none -> 7.44 us  [body(): lax.all_to_all(jnp.stack([copies] * lax.axis_size(('keys', 'qry'))), ('ke...]
    psum x1, blocking collectives: 31.9 us -> 35.4 us  [body(): squares_all = lax.psum(squared_terms, ('keys', 'qry'))]
    another operation x8 -> x9, local copies, waits for them, and re-layouts: 3.92 us -> 4.81 us
  transfers between devices with their start and end apart: 7 -> 8, of which waited for: 1 -> 1; matrix products, arithmetic and copies ran while one was open for 15% -> 22% of each run, Pallas kernels for 0% -> 0%
where the time goes in v1:
time: 137 us; the launch traced here: 136 us
  blocking collectives  35.4 us (26%)
  waiting for transfers between devices  23.4 us (17%)
  matrix products  23.3 us (17%)
  between operations  17.3 us (13%)
  other arithmetic  12.6 us (9%)
  starting transfers between devices  10.1 us (7%)
  local copies, waits for them, and re-layouts  8.09 us (6%)
  loops' own time  6.18 us (5%)
    psum x1, blocking collectives, body(): squares_all = lax.psum(squared_terms, ('keys', 'qry'))  35.4 us
    reduce_scatter x1, waiting for transfers between devices, body(): lax.psum_scatter(grad_terms, ('keys', 'qry'), scatter_dimension=0, tiled=...  23.3 us
    dot_general x12, matrix products, row_scores(): lax.dot_general(left, right, (((1,), (1,)), ((), ())), preferred_element_...  10.1 us
    dot_general x8, matrix products, one(): jnp.dot(weight.astype(jnp.bfloat16), values, preferred_element_type=jnp.f...  9.4 us
    all_to_all x1, starting transfers between devices, body(): lax.all_to_all(jnp.stack([copies] * lax.axis_size(('keys', 'qry'))), ('ke...  7.44 us
    lt x8, other arithmetic, attend(): live = (place < length)[None, :]  5.37 us
    another operation x1, loops' own time, body(): lax.fori_loop(0, shards - 1, turn, (cache_keys, cache_values) + state)  4.07 us
    another operation x8, local copies, waits for them, and re-layouts  3.95 us
  transfers between devices with their start and end apart: 8, of which 1 were waited for; matrix products, arithmetic and copies ran while one was open for 22% of the time, Pallas kernels for 0%

profile of v1, /device:TPU:0, one launch (start us, length us, event | category | flops | bytes accessed | tf_op | source)
XLA Modules:
  0.0 136.3 jit_solution(1396407432588504097)
XLA Ops:
  7.2 0.9 convert_element_type.42
  9.0 7.4 %all-to-all-start = ((bf16[16,64,256]{2,1,0:T(8,128)(2,1)}), bf16[16,64,256]{2,1,0:T(8,128)(2,1)}, u32[]{:S(2)}, u32[]{:S(2)}) async-start(bf16[16,64,256]{2,1,0:T(8,128)(2,1)} %stack.2), calls=%async_computation | async-start | bytes 1048576 | tf_op jit(solution)/shard_map/all_to_all | solution.py:122
  17.9 33.1 %while.82 = (s32[]{:T(128)}, bf16[512,128]{1,0:T(8,128)(2,1)S(1)}, bf16[512,128]{1,0:T(8,128)(2,1)S(1)}, f32[2,512]{1,0:T(2,128)S(1)}, f32[2,512]{1,0:T(2,128)S(...) while((s32[]{:T(128)}, bf16[512,128]{1,0:T(8,128)(2,1)S(1)}, ...), condition=%wide.region_7.8_spmd, body=%wide.region_0.7_spmd.sunk | while | flops 136711200 | bytes 6747030 | solution.py:114
  19.6 1.6 %collective-permute-start.1 = (bf16[512,128]{1,0:T(8,128)(2,1)}, bf16[512,128]{1,0:T(8,128)(2,1)S(1)}, u32[]{:S(2)}, u32[]{:S(2)}) collective-permute-start(bf16[512,128]{1,0:T(8,128)(2,1)} %copy.56), channel_id=1, source_target_pairs={{12,0},{0,4},{4,8},{8,12},{13,1},{1,5},{5,9},{9,13},{14,2},{2,6},{... | collective-permute-start | bytes 393224 | tf_op jit(solution)/shard_map/while/body/eval_jaxpr/ppermute | solution.py:13
  22.5 7.5 %conditional.4 = ((f32[2,512]{1,0:T(2,128)S(1)}, f32[2,512]{1,0:T(2,128)S(1)}, f32[2,512,128]{2,1,0:T(8,128)S(1)})) conditional(s32[]{:T(128)} %convert_element_type.75, (f32[2,512]{1,0:T(2,128)S(1)}, f32[2,512]{1,0:T(2,128)S(1)}, f32[2,512,128]{2,1,0:T(8,128)S(1)}) %tuple.135, (s32[]{:T(128)}, s32[]{:T(128)}, s32[]{:T(128)}, f32[2,512]{1,0:T(2,128)S(1)}, ...), branch_computations={%region_1.1_spmd, %region_2.6_spmd} | conditional | flops 136711184 | bytes 5173698 | solution.py:99
  22.6 7.4 %while.80 = (s32[]{:T(128)}, f32[2,512]{1,0:T(2,128)S(1)}, f32[2,512]{1,0:T(2,128)S(1)}, f32[2,512,128]{2,1,0:T(8,128)S(1)}, f32[2,512]{1,0:T(2,128)S(1)}, /*ind...) while((s32[]{:T(128)}, f32[2,512]{1,0:T(2,128)S(1)}, ...), condition=%wide.region_6.5_spmd.clone, body=%wide.region_3.4_spmd.clone.sunk | while | flops 136711168 | bytes 4108453 | solution.py:40
  23.3 1.2 fusion.104
  24.5 1.4 %fusion.106 = f32[2,512,128]{2,1,0:T(8,128)S(1)} fusion(f32[2,512,128]{2,1,0:T(8,128)S(1)} %get-tuple-element.1145, s32[]{:T(128)} %get-tuple-element.1142, bf16[512,128]{1,0:T(8,128)(2,1)} %get-tuple-element.1165, f32[512,512]{0,1:T(8,128)S(1)} %get-tuple-element.1107, f32[512]{0:T(512)S(1)} %get-tuple-element.1109, ...), kind=kOutput, calls=%fused_computation.32.clone.1 | convolution fusion | flops 68026368 | bytes 1708548 | tf_op jit(solution)/shard_map/while/body/eval_jaxpr/cond/branch_1_fun/while/body/eval_jaxpr/dot_general | solution.py:34
  26.9 1.2 fusion.104
  28.2 1.4 %fusion.106 = f32[2,512,128]{2,1,0:T(8,128)S(1)} fusion(f32[2,512,128]{2,1,0:T(8,128)S(1)} %get-tuple-element.1145, s32[]{:T(128)} %get-tuple-element.1142, bf16[512,128]{1,0:T(8,128)(2,1)} %get-tuple-element.1165, f32[512,512]{0,1:T(8,128)S(1)} %get-tuple-element.1107, f32[512]{0:T(512)S(1)} %get-tuple-element.1109, ...), kind=kOutput, calls=%fused_computation.32.clone.1 | convolution fusion | flops 68026368 | bytes 1708548 | tf_op jit(solution)/shard_map/while/body/eval_jaxpr/cond/branch_1_fun/while/body/eval_jaxpr/dot_general | solution.py:34
  32.9 7.5 %conditional.4 = ((f32[2,512]{1,0:T(2,128)S(1)}, f32[2,512]{1,0:T(2,128)S(1)}, f32[2,512,128]{2,1,0:T(8,128)S(1)})) conditional(s32[]{:T(128)} %convert_element_type.75, (f32[2,512]{1,0:T(2,128)S(1)}, f32[2,512]{1,0:T(2,128)S(1)}, f32[2,512,128]{2,1,0:T(8,128)S(1)}) %tuple.135, (s32[]{:T(128)}, s32[]{:T(128)}, s32[]{:T(128)}, f32[2,512]{1,0:T(2,128)S(1)}, ...), branch_computations={%region_1.1_spmd, %region_2.6_spmd} | conditional | flops 136711184 | bytes 5173698 | solution.py:99
  33.0 7.4 %while.80 = (s32[]{:T(128)}, f32[2,512]{1,0:T(2,128)S(1)}, f32[2,512]{1,0:T(2,128)S(1)}, f32[2,512,128]{2,1,0:T(8,128)S(1)}, f32[2,512]{1,0:T(2,128)S(1)}, /*ind...) while((s32[]{:T(128)}, f32[2,512]{1,0:T(2,128)S(1)}, ...), condition=%wide.region_6.5_spmd.clone, body=%wide.region_3.4_spmd.clone.sunk | while | flops 136711168 | bytes 4108453 | solution.py:40
  33.7 1.2 fusion.104
  34.9 1.4 %fusion.106 = f32[2,512,128]{2,1,0:T(8,128)S(1)} fusion(f32[2,512,128]{2,1,0:T(8,128)S(1)} %get-tuple-element.1145, s32[]{:T(128)} %get-tuple-element.1142, bf16[512,128]{1,0:T(8,128)(2,1)} %get-tuple-element.1165, f32[512,512]{0,1:T(8,128)S(1)} %get-tuple-element.1107, f32[512]{0:T(512)S(1)} %get-tuple-element.1109, ...), kind=kOutput, calls=%fused_computation.32.clone.1 | convolution fusion | flops 68026368 | bytes 1708548 | tf_op jit(solution)/shard_map/while/body/eval_jaxpr/cond/branch_1_fun/while/body/eval_jaxpr/dot_general | solution.py:34
  37.4 1.2 fusion.104
  38.6 1.4 %fusion.106 = f32[2,512,128]{2,1,0:T(8,128)S(1)} fusion(f32[2,512,128]{2,1,0:T(8,128)S(1)} %get-tuple-element.1145, s32[]{:T(128)} %get-tuple-element.1142, bf16[512,128]{1,0:T(8,128)(2,1)} %get-tuple-element.1165, f32[512,512]{0,1:T(8,128)S(1)} %get-tuple-element.1107, f32[512]{0:T(512)S(1)} %get-tuple-element.1109, ...), kind=kOutput, calls=%fused_computation.32.clone.1 | convolution fusion | flops 68026368 | bytes 1708548 | tf_op jit(solution)/shard_map/while/body/eval_jaxpr/cond/branch_1_fun/while/body/eval_jaxpr/dot_general | solution.py:34
  43.4 7.5 %conditional.4 = ((f32[2,512]{1,0:T(2,128)S(1)}, f32[2,512]{1,0:T(2,128)S(1)}, f32[2,512,128]{2,1,0:T(8,128)S(1)})) conditional(s32[]{:T(128)} %convert_element_type.75, (f32[2,512]{1,0:T(2,128)S(1)}, f32[2,512]{1,0:T(2,128)S(1)}, f32[2,512,128]{2,1,0:T(8,128)S(1)}) %tuple.135, (s32[]{:T(128)}, s32[]{:T(128)}, s32[]{:T(128)}, f32[2,512]{1,0:T(2,128)S(1)}, ...), branch_computations={%region_1.1_spmd, %region_2.6_spmd} | conditional | flops 136711184 | bytes 5173698 | solution.py:99
  43.5 7.4 %while.80 = (s32[]{:T(128)}, f32[2,512]{1,0:T(2,128)S(1)}, f32[2,512]{1,0:T(2,128)S(1)}, f32[2,512,128]{2,1,0:T(8,128)S(1)}, f32[2,512]{1,0:T(2,128)S(1)}, /*ind...) while((s32[]{:T(128)}, f32[2,512]{1,0:T(2,128)S(1)}, ...), condition=%wide.region_6.5_spmd.clone, body=%wide.region_3.4_spmd.clone.sunk | while | flops 136711168 | bytes 4108453 | solution.py:40
  44.2 1.2 fusion.104
  45.5 1.4 %fusion.106 = f32[2,512,128]{2,1,0:T(8,128)S(1)} fusion(f32[2,512,128]{2,1,0:T(8,128)S(1)} %get-tuple-element.1145, s32[]{:T(128)} %get-tuple-element.1142, bf16[512,128]{1,0:T(8,128)(2,1)} %get-tuple-element.1165, f32[512,512]{0,1:T(8,128)S(1)} %get-tuple-element.1107, f32[512]{0:T(512)S(1)} %get-tuple-element.1109, ...), kind=kOutput, calls=%fused_computation.32.clone.1 | convolution fusion | flops 68026368 | bytes 1708548 | tf_op jit(solution)/shard_map/while/body/eval_jaxpr/cond/branch_1_fun/while/body/eval_jaxpr/dot_general | solution.py:34
  47.9 1.2 fusion.104
  49.1 1.4 %fusion.106 = f32[2,512,128]{2,1,0:T(8,128)S(1)} fusion(f32[2,512,128]{2,1,0:T(8,128)S(1)} %get-tuple-element.1145, s32[]{:T(128)} %get-tuple-element.1142, bf16[512,128]{1,0:T(8,128)(2,1)} %get-tuple-element.1165, f32[512,512]{0,1:T(8,128)S(1)} %get-tuple-element.1107, f32[512]{0:T(512)S(1)} %get-tuple-element.1109, ...), kind=kOutput, calls=%fused_computation.32.clone.1 | convolution fusion | flops 68026368 | bytes 1708548 | tf_op jit(solution)/shard_map/while/body/eval_jaxpr/cond/branch_1_fun/while/body/eval_jaxpr/dot_general | solution.py:34
  51.0 3.8 %conditional.2 = ((f32[2,512]{1,0:T(2,128)S(1)}, f32[2,512,128]{2,1,0:T(8,128)S(1)})) conditional(s32[]{:T(128)} %convert_element_type.40, (f32[2,512]{1,0:T(2,128)S(1)}, f32[2,512,128]{2,1,0:T(8,128)S(1)}) %tuple.70, (s32[]{:T(128)}, s32[]{:T(128)}, f32[2,512]{1,0:T(2,128)S(1)}, f32[2,512]{1,0:T(2,128)S(1)}, bf16[2,512,128]{2,1,0:T(8,128)(2,1)S(1)}, ...), branch_computations={%region_8.9_spmd, %region_9.14_spmd} | conditional | flops 136711184 | bytes 5159334 | solution.py:99
  51.0 3.7 %while.81 = (s32[]{:T(128)}, f32[2,512]{1,0:T(2,128)S(1)}, f32[2,512,128]{2,1,0:T(8,128)S(1)}, f32[2,512]{1,0:T(2,128)S(1)}, f32[2,512]{1,0:T(2,128)S(1)}, /*ind...) while((s32[]{:T(128)}, f32[2,512]{1,0:T(2,128)S(1)}, ...), condition=%wide.region_13.13_spmd.clone, body=%wide.region_10.12_spmd.clone.sunk | while | flops 136711168 | bytes 4102297 | solution.py:40
  55.0 1.1 fusion.56
  56.1 10.0 %while.83 = (s32[]{:T(128)}, f32[1024,256]{0,1:T(8,128)S(1)}, f32[]{:T(128)}, bf16[2,512,128]{2,1,0:T(8,128)(2,1)S(1)}, bf16[1024,128]{1,0:T(8,128)(2,1)S(1)}, /...) while((s32[]{:T(128)}, f32[1024,256]{0,1:T(8,128)S(1)}, ...), condition=%wide.region_19.20_spmd.clone, body=%wide.region_14.19_spmd.clone.sunk | while | flops 680589824 | bytes 26753152 | solution.py:128
  57.6 1.1 multiply_reduce_fusion.7
  62.6 1.1 multiply_reduce_fusion.7
  66.1 1.3 copy.15
  67.5 35.4 %psum.7 = f32[]{:T(128)} all-reduce(f32[]{:T(128)} %get-tuple-element.654), channel_id=1, replica_groups=mesh['grp'=2,'keys'=4,'qry'=4] {'keys','qry'}, use_global_device_ids=true, to_apply=%region_21.22 | all-reduce | flops 1 | bytes 8 | tf_op jit(solution)/shard_map/psum | solution.py:136
  103.5 23.3 %reduce-scatter.2.cloned.1.call-done = f32[64,256]{1,0:T(8,128)} async-done(((f32[1024,256]{1,0:T(8,128)}), f32[64,256]{1,0:T(8,128)}) %reduce-scatter.2.cloned.1.call-update) | async-done | bytes 65552 | tf_op jit(solution)/shard_map/reduce_scatter | solution.py:135
  126.8 1.5 %divide_subtract_fusion = (f32[64,256]{1,0:T(8,128)}, f32[64,256]{1,0:T(8,128)}, f32[64,256]{1,0:T(8,128)}) fusion(f32[64,256]{1,0:T(8,128)S(1)} %copy-done.4, f32[64,256]{1,0:T(8,128)} %reduce-scatter.2.cloned.1.call-done, f32[64,256]{1,0:T(8,128)S(1)} %copy-done.5, f32[64,256]{1,0:T(8,128)S(1)} %copy-done.6), kind=kLoop, calls=%fused_computation.74 | loop fusion | flops 180224 | bytes 458752 | tf_op jit(solution)/shard_map/sub | solution.py:140
  (134 shorter events, 22.4 us)
Async XLA Ops:
  7.2 10.7 %copy-start = (bf16[128,8,128]{2,1,0:T(8,128)(2,1)S(1)}, bf16[128,8,128]{2,1,0:T(8,128)(2,1)}, u32[]{:S(2)}) copy-start(bf16[128,8,128]{2,1,0:T(8,128)(2,1)} %param.21) | copy-start | bytes 786436
  7.2 10.7 %copy-start.1 = (bf16[512,128]{1,0:T(8,128)(2,1)S(1)}, bf16[512,128]{1,0:T(8,128)(2,1)}, u32[]{:S(2)}) copy-start(bf16[512,128]{1,0:T(8,128)(2,1)} %param.22) | copy-start | bytes 393220
  7.2 10.7 %copy-start.2 = (bf16[512,128]{1,0:T(8,128)(2,1)S(1)}, bf16[512,128]{1,0:T(8,128)(2,1)}, u32[]{:S(2)}) copy-start(bf16[512,128]{1,0:T(8,128)(2,1)} %param.23) | copy-start | bytes 393220
  9.0 46.0 %all-to-all-start = ((bf16[16,64,256]{2,1,0:T(8,128)(2,1)}), bf16[16,64,256]{2,1,0:T(8,128)(2,1)}, u32[]{:S(2)}, u32[]{:S(2)}) async-start(bf16[16,64,256]{2,1,0:T(8,128)(2,1)} %stack.2), calls=%async_computation | async-start | bytes 1048576 | tf_op jit(solution)/shard_map/all_to_all | solution.py:122
  16.4 110.4 %reduce-scatter.2.cloned.1.call-start = ((), (), s32[]{:S(2)}) async-start(), calls=%async_computation.2 | async-start | bytes 1114112 | tf_op jit(solution)/shard_map/reduce_scatter | solution.py:135
  18.6 11.4 %collective-permute-start = (bf16[512,128]{1,0:T(8,128)(2,1)}, bf16[512,128]{1,0:T(8,128)(2,1)S(1)}, u32[]{:S(2)}, u32[]{:S(2)}) collective-permute-start(bf16[512,128]{1,0:T(8,128)(2,1)} %copy.55), channel_id=1, source_target_pairs={{12,0},{0,4},{4,8},{8,12},{13,1},{1,5},{5,9},{9,13},{14,2},{2,6},{... | collective-permute-start | bytes 393224 | tf_op jit(solution)/shard_map/while/body/eval_jaxpr/ppermute | solution.py:13
  19.6 10.5 %collective-permute-start.1 = (bf16[512,128]{1,0:T(8,128)(2,1)}, bf16[512,128]{1,0:T(8,128)(2,1)S(1)}, u32[]{:S(2)}, u32[]{:S(2)}) collective-permute-start(bf16[512,128]{1,0:T(8,128)(2,1)} %copy.56), channel_id=1, source_target_pairs={{12,0},{0,4},{4,8},{8,12},{13,1},{1,5},{5,9},{9,13},{14,2},{2,6},{... | collective-permute-start | bytes 393224 | tf_op jit(solution)/shard_map/while/body/eval_jaxpr/ppermute | solution.py:13
  30.7 9.7 %collective-permute-start = (bf16[512,128]{1,0:T(8,128)(2,1)}, bf16[512,128]{1,0:T(8,128)(2,1)S(1)}, u32[]{:S(2)}, u32[]{:S(2)}) collective-permute-start(bf16[512,128]{1,0:T(8,128)(2,1)} %copy.55), channel_id=1, source_target_pairs={{12,0},{0,4},{4,8},{8,12},{13,1},{1,5},{5,9},{9,13},{14,2},{2,6},{... | collective-permute-start | bytes 393224 | tf_op jit(solution)/shard_map/while/body/eval_jaxpr/ppermute | solution.py:13
  31.5 9.0 %collective-permute-start.1 = (bf16[512,128]{1,0:T(8,128)(2,1)}, bf16[512,128]{1,0:T(8,128)(2,1)S(1)}, u32[]{:S(2)}, u32[]{:S(2)}) collective-permute-start(bf16[512,128]{1,0:T(8,128)(2,1)} %copy.56), channel_id=1, source_target_pairs={{12,0},{0,4},{4,8},{8,12},{13,1},{1,5},{5,9},{9,13},{14,2},{2,6},{... | collective-permute-start | bytes 393224 | tf_op jit(solution)/shard_map/while/body/eval_jaxpr/ppermute | solution.py:13
  41.1 9.8 %collective-permute-start = (bf16[512,128]{1,0:T(8,128)(2,1)}, bf16[512,128]{1,0:T(8,128)(2,1)S(1)}, u32[]{:S(2)}, u32[]{:S(2)}) collective-permute-start(bf16[512,128]{1,0:T(8,128)(2,1)} %copy.55), channel_id=1, source_target_pairs={{12,0},{0,4},{4,8},{8,12},{13,1},{1,5},{5,9},{9,13},{14,2},{2,6},{... | collective-permute-start | bytes 393224 | tf_op jit(solution)/shard_map/while/body/eval_jaxpr/ppermute | solution.py:13
  42.1 8.8 %collective-permute-start.1 = (bf16[512,128]{1,0:T(8,128)(2,1)}, bf16[512,128]{1,0:T(8,128)(2,1)S(1)}, u32[]{:S(2)}, u32[]{:S(2)}) collective-permute-start(bf16[512,128]{1,0:T(8,128)(2,1)} %copy.56), channel_id=1, source_target_pairs={{12,0},{0,4},{4,8},{8,12},{13,1},{1,5},{5,9},{9,13},{14,2},{2,6},{... | collective-permute-start | bytes 393224 | tf_op jit(solution)/shard_map/while/body/eval_jaxpr/ppermute | solution.py:13
  66.1 62.3 %copy-start.3 = (bf16[2,512,128]{2,1,0:T(8,128)(2,1)}, bf16[2,512,128]{2,1,0:T(8,128)(2,1)S(1)}, u32[]{:S(2)}) copy-start(bf16[2,512,128]{2,1,0:T(8,128)(2,1)S(1)} %get-tuple-element.1306) | copy-start | bytes 786436
  66.1 60.8 %copy-start.4 = (f32[64,256]{1,0:T(8,128)S(1)}, f32[64,256]{1,0:T(8,128)}, u32[]{:S(2)}) copy-start(f32[64,256]{1,0:T(8,128)} %param.27) | copy-start | bytes 196612
  66.1 60.8 %copy-start.5 = (f32[64,256]{1,0:T(8,128)S(1)}, f32[64,256]{1,0:T(8,128)}, u32[]{:S(2)}) copy-start(f32[64,256]{1,0:T(8,128)} %param.28) | copy-start | bytes 196612
  66.1 60.7 %copy-start.6 = (f32[64,256]{1,0:T(8,128)S(1)}, f32[64,256]{1,0:T(8,128)}, u32[]{:S(2)}) copy-start(f32[64,256]{1,0:T(8,128)} %param.29) | copy-start | bytes 196612
Sparse Core Ops, SparseCore 0:
  67.6 59.2 reduce-scatter.1
